TPU v7x, 32 devices: a whole 2x2x4 slice. The times are simulated.
32 devices in a mesh: enc: 2 (over core), dp: 4 (over z), mp: 4 (over y, x).
Axes of the slice: x: 2, y: 2, z: 4, core: 2. Of those that a mesh axis runs over, the one named last changes fastest.
Arguments:
- token_ids: int32 [2, 16, 256], P('enc', 'dp'), may hold values from 0 to 30719
- query_lengths: int32 [32], P('dp'), may hold values from 1 to 128, 2048 in all
- negative_mask: int32 [32, 16], replicated, may hold values 0 or 1
- positive_index: int32 [32], replicated, may hold values from 0 to 15
- used_rows: int32 [32], replicated, may hold values 0 or 1
- step_count: int32 [1], replicated, may hold values from 2 to 20
- table: float32 [2, 30720, 768], P('enc', ('dp', 'mp')), may hold values from -0.18 to 0.18
- w_mixed: float32 [2, 768, 3, 768], P('enc', 'dp', None, 'mp'), may hold values from -0.21875 to 0.21875
- w_out: float32 [2, 768, 768], P('enc', 'mp', 'dp'), may hold values from -0.875 to 0.875
- w_inner: float32 [2, 768, 3072], P('enc', 'dp', 'mp'), may hold values from -0.21875 to 0.21875
- w_outer: float32 [2, 3072, 768], P('enc', 'mp', 'dp'), may hold values from -0.109375 to 0.109375
- norm_params: float32 [2, 6, 768], P('enc'), as said below
- table_m: float32 [2, 30720, 768], P('enc', ('dp', 'mp')), may hold values from -1.1234977e-06 to 1.1234977e-06
- table_v: float32 [2, 30720, 768], P('enc', ('dp', 'mp')), may hold values from 6.5198705e-15 to 2.6079482e-14
- mixed_m: float32 [2, 768, 3, 768], P('enc', 'dp', None, 'mp'), may hold values from -1.1234977e-06 to 1.1234977e-06
- mixed_v: float32 [2, 768, 3, 768], P('enc', 'dp', None, 'mp'), may hold values from 6.5198705e-15 to 2.6079482e-14
- out_m: float32 [2, 768, 768], P('enc', 'mp', 'dp'), may hold values from -1.1234977e-06 to 1.1234977e-06
- out_v: float32 [2, 768, 768], P('enc', 'mp', 'dp'), may hold values from 6.5198705e-15 to 2.6079482e-14
- inner_m: float32 [2, 768, 3072], P('enc', 'dp', 'mp'), may hold values from -1.1234977e-06 to 1.1234977e-06
- inner_v: float32 [2, 768, 3072], P('enc', 'dp', 'mp'), may hold values from 6.5198705e-15 to 2.6079482e-14
- outer_m: float32 [2, 3072, 768], P('enc', 'mp', 'dp'), may hold values from -1.1234977e-06 to 1.1234977e-06
- outer_v: float32 [2, 3072, 768], P('enc', 'mp', 'dp'), may hold values from 6.5198705e-15 to 2.6079482e-14
- norms_m: float32 [2, 6, 768], P('enc'), may hold values from -4.4684566e-06 to 4.4684566e-06
- norms_v: float32 [2, 6, 768], P('enc'), may hold values from 1.0431793e-13 to 4.172717e-13
Outputs:
- loss: float32 [], replicated
- grad_norm: float32 [], replicated
- table_new: float32 [2, 30720, 768], P('enc', ('dp', 'mp'))
- table_m_new: float32 [2, 30720, 768], P('enc', ('dp', 'mp'))
- table_v_new: float32 [2, 30720, 768], P('enc', ('dp', 'mp'))
- mixed_new: float32 [2, 768, 3, 768], P('enc', 'dp', None, 'mp')
- mixed_m_new: float32 [2, 768, 3, 768], P('enc', 'dp', None, 'mp')
- mixed_v_new: float32 [2, 768, 3, 768], P('enc', 'dp', None, 'mp')
- out_new: float32 [2, 768, 768], P('enc', 'mp', 'dp')
- out_m_new: float32 [2, 768, 768], P('enc', 'mp', 'dp')
- output_second_moment_next: float32 [2, 768, 768], P('enc', 'mp', 'dp')
- inner_new: float32 [2, 768, 3072], P('enc', 'dp', 'mp')
- inner_m_new: float32 [2, 768, 3072], P('enc', 'dp', 'mp')
- inner_v_new: float32 [2, 768, 3072], P('enc', 'dp', 'mp')
- outer_new: float32 [2, 3072, 768], P('enc', 'mp', 'dp')
- outer_m_new: float32 [2, 3072, 768], P('enc', 'mp', 'dp')
- outer_v_new: float32 [2, 3072, 768], P('enc', 'mp', 'dp')
- norms_new: float32 [2, 6, 768], P('enc')
- norms_m_new: float32 [2, 6, 768], P('enc')
- norms_v_new: float32 [2, 6, 768], P('enc')
Inputs may be any that keep to these rules, and one draw needn't show every extreme that they name: `norm_params`: gains (rows 0, 2, 4) lie in 0.7 to 1.3, shifts (rows 1, 3, 5) are small.
All inputs are finite; a program needn't handle non-finite values. No bound on the sum of `query_lengths` on one device may be relied on, other than what follows from the above.
Results may differ from a plain program's by a relative error of at most 0.015.
Values may be sent and summed in bfloat16 or wider, within the bound.
A program may use at most 192 MiB of HBM per device.

v0:
```python
from functools import partial
import jax
import jax.numpy as jnp
from jax import lax
from jax.sharding import PartitionSpec as P

HEAD = 64
QSLOT = 128
F32 = jnp.float32
BF16 = jnp.bfloat16
exact_arithmetic_level = lax.Precision.HIGHEST
eps_norm = 1e-06
logit_divisor = 0.05
clip_limit = 0.02
beta_one = 0.9
beta_two = 0.999
adam_eps = 1e-08


def layer_norm(x, gain, shift):
    centred = x - jnp.mean(x, -1, keepdims=True)
    spread = jnp.mean(centred * centred, -1, keepdims=True)
    return centred * lax.rsqrt(spread + eps_norm) * gain + shift


def mul(spec, a, b):
    return jnp.einsum(spec, a, b, preferred_element_type=F32)


def token_counts(ids, lens, is_query, base, rows):
    pos = jnp.arange(ids.shape[1])
    slot = pos // QSLOT
    limit = jnp.where(slot[None, :] == 0, lens[:, 0:1], lens[:, 1:2])
    within = (pos % QSLOT)[None, :] < limit
    same = slot[None, :] == jnp.arange(2)[:, None]
    allowed = jnp.where(is_query, same[:, None, :] & within[None], True)
    local = ids - base
    n_hi = -(-rows // 128)
    high = local[..., None] >> 7 == jnp.arange(n_hi)
    low = local[..., None] & 127 == jnp.arange(128)
    left = (allowed[..., None] & high[None]).astype(BF16)
    counts = mul("sbth,btl->sbhl", left, low.astype(BF16))
    return counts.reshape(2 * ids.shape[0], n_hi * 128)[:, :rows]


def contrast(queries, passages, negative_mask, positive_index, used_rows):
    question_direction_rows = queries * lax.rsqrt(
        jnp.sum(queries * queries, -1, keepdims=True) + eps_norm
    )
    document_direction_rows = passages * lax.rsqrt(
        jnp.sum(passages * passages, -1, keepdims=True) + eps_norm
    )
    pairwise_cosine_table = (
        jnp.dot(
            question_direction_rows, document_direction_rows.T, precision=exact_arithmetic_level
        )
        / logit_divisor
    )
    is_positive = jnp.arange(passages.shape[0])[None, :] == positive_index[:, None]
    excluded = (negative_mask == 1) & ~is_positive
    pairwise_cosine_table = jnp.where(excluded, -1e30, pairwise_cosine_table)
    top = jnp.max(pairwise_cosine_table, -1, keepdims=True)
    log_total = top[:, 0] + jnp.log(jnp.sum(jnp.exp(pairwise_cosine_table - top), -1))
    target = jnp.sum(jnp.where(is_positive, pairwise_cosine_table, 0.0), -1)
    weight = used_rows.astype(F32)
    return jnp.sum(weight * (log_total - target)) / jnp.maximum(jnp.sum(weight), 1.0)


def adam_step(weight, grad, first, second, rate, decay, count):
    first_new = beta_one * first + (1.0 - beta_one) * grad
    second_new = beta_two * second + (1.0 - beta_two) * grad * grad
    fix_one = 1.0 - jnp.power(beta_one, count)
    correction_second = 1.0 - jnp.power(beta_two, count)
    update = (
        first_new / fix_one / (jnp.sqrt(second_new / correction_second) + adam_eps) + decay * weight
    )
    return (weight - rate * update, first_new, second_new)


def slot_major(x):
    return x.reshape((x.shape[0] // 2, 2) + x.shape[1:]).swapaxes(0, 1).reshape(x.shape)


def gradients(
    token_ids,
    query_lengths,
    negative_mask,
    positive_index,
    used_rows,
    table,
    w_mixed,
    w_out,
    w_inner,
    w_outer,
    norm_params,
):
    is_query = lax.axis_index("enc") == 0
    d, m = (lax.axis_index("dp"), lax.axis_index("mp"))
    n_mp = lax.axis_size("mp")
    rows, width = (table.shape[1], w_mixed.shape[1])
    hm = w_out.shape[1] // HEAD
    scale = HEAD ** (-0.5)
    norms = norm_params[0]
    base = (d * n_mp + m) * rows
    ids = lax.all_gather(token_ids[0], "dp", axis=0, tiled=True)
    lens = lax.all_gather(query_lengths, "dp", axis=0, tiled=True).reshape(-1, 2)
    blocks = ids.shape[0]
    counts = token_counts(ids, lens, is_query, base, rows)
    cls_ids = jnp.concatenate([ids[:, 0], ids[:, QSLOT]]) - base
    cls_hot = cls_ids[:, None] == jnp.arange(rows)[None, :]

    def mine(x):
        return lax.dynamic_slice_in_dim(x, d * width, width, 1)

    wq, wk, wv = (w_mixed[0, :, i].astype(BF16).reshape(width, hm, HEAD) for i in range(3))
    wo = w_out[0].astype(BF16).reshape(hm, HEAD, width)
    wi, wt = (w_inner[0].astype(BF16), w_outer[0].astype(BF16))
    embedded = lax.reduce_precision(table[0], 8, 7)
    hidden, hidden_back = jax.vjp(layer_norm, embedded, norms[0], norms[1])
    hid = hidden.astype(BF16)
    first_rows = lax.psum(
        jnp.dot(cls_hot.astype(F32), hidden, precision=exact_arithmetic_level), ("dp", "mp")
    )
    first_mine = mine(first_rows).astype(BF16)
    q = lax.psum(mul("ci,ihk->hck", first_mine, wq), "dp").astype(BF16)
    u = mul("hck,ihk->hci", q, wk).astype(BF16)
    u = lax.all_gather(lax.all_gather(u, "dp", axis=2, tiled=True), "mp", axis=0, tiled=True)
    scores = jnp.where(counts[None] > 0, mul("hci,vi->hcv", u, hid) * scale, -1e30)
    top = lax.pmax(jnp.max(scores, -1, keepdims=True), ("dp", "mp"))
    weight = counts[None] * jnp.exp(scores - top)
    probs = weight / lax.psum(jnp.sum(weight, -1, keepdims=True), ("dp", "mp"))
    probs_low = probs.astype(BF16)
    z = mul("hcv,vi->hci", probs_low, hid)
    z = lax.psum_scatter(z, "mp", scatter_dimension=0, tiled=True)
    z = lax.psum_scatter(z, "dp", scatter_dimension=2, tiled=True).astype(BF16)
    att = lax.psum(mul("hci,ihk->hck", z, wv), "dp")
    att_low = att.astype(BF16)
    out = lax.psum(mul("hck,hke->ce", att_low, wo), "mp")
    first_sum = first_rows + lax.all_gather(out, "dp", axis=1, tiled=True)
    normed, normed_back = jax.vjp(layer_norm, first_sum, norms[2], norms[3])
    normed_mine = mine(normed).astype(BF16)
    inner = lax.psum(mul("ci,if->cf", normed_mine, wi), "dp")
    act, act_back = jax.vjp(partial(jax.nn.gelu, approximate=False), inner)
    act = act.astype(BF16)
    outer = lax.psum(mul("cf,fe->ce", act, wt), "mp")
    second_sum = normed + lax.all_gather(outer, "dp", axis=1, tiled=True)
    final, final_back = jax.vjp(layer_norm, second_sum, norms[4], norms[5])
    both = lax.all_gather(final, "enc", axis=0)
    loss, loss_back = jax.vjp(
        partial(
            contrast,
            negative_mask=slot_major(negative_mask),
            positive_index=slot_major(positive_index),
            used_rows=slot_major(used_rows),
        ),
        both[0],
        both[1, :blocks],
    )
    d_queries, d_passages = loss_back(jnp.ones((), F32))
    d_passages = jnp.concatenate([d_passages, jnp.zeros_like(d_passages)])
    d_final = jnp.where(is_query, d_queries, d_passages)
    d_second, d_gain2, d_shift2 = final_back(d_final)
    d_outer = mine(d_second).astype(BF16)
    g_outer = mul("cf,ce->fe", act, d_outer)
    d_act = lax.psum(mul("ce,fe->cf", d_outer, wt), "dp")
    d_inner = act_back(d_act)[0].astype(BF16)
    g_inner = mul("ci,cf->if", normed_mine, d_inner)
    d_in = lax.psum(mul("cf,if->ci", d_inner, wi), "mp")
    d_normed = d_second + lax.all_gather(d_in, "dp", axis=1, tiled=True)
    d_first, d_gain1, d_shift1 = normed_back(d_normed)
    d_attn = mine(d_first).astype(BF16)
    g_out = mul("hck,ce->hke", att_low, d_attn).reshape(w_out.shape[1:])
    d_att = lax.psum(mul("ce,hke->hck", d_attn, wo), "dp").astype(BF16)
    w = mul("hck,ihk->hci", d_att, wv).astype(BF16)
    mean_d = jnp.sum(att * d_att.astype(F32), -1, keepdims=True)
    w = lax.all_gather(lax.all_gather(w, "dp", axis=2, tiled=True), "mp", axis=0, tiled=True)
    mean_d = lax.all_gather(mean_d, "mp", axis=0, tiled=True)
    d_probs = mul("hci,vi->hcv", w, hid)
    d_scores = (probs * (d_probs - mean_d)).astype(BF16)
    y = mul("hcv,vi->hci", d_scores, hid)
    y = lax.psum_scatter(y, "mp", scatter_dimension=0, tiled=True)
    y = lax.psum_scatter(y, "dp", scatter_dimension=2, tiled=True).astype(BF16)
    dq = (lax.psum(mul("hci,ihk->hck", y, wk), "dp") * scale).astype(BF16)
    g_q = mul("ci,hck->ihk", first_mine, dq)
    g_k = mul("hci,hck->ihk", y, q) * scale
    g_v = mul("hci,hck->ihk", z, d_att)
    g_mixed = jnp.stack([g_q, g_k, g_v], 1).reshape(w_mixed.shape[1:])
    d_rows = lax.psum(mul("hck,ihk->ci", dq, wq), "mp")
    d_rows = (d_first + lax.all_gather(d_rows, "dp", axis=1, tiled=True)).astype(BF16)
    d_hidden = (
        mul("hcv,hci->vi", d_scores, u) * scale
        + mul("hcv,hci->vi", probs_low, w)
        + mul("cv,ci->vi", cls_hot.astype(BF16), d_rows)
    )
    g_table, d_gain0, d_shift0 = hidden_back(d_hidden)
    sums = lax.psum(jnp.stack([d_gain0, d_shift0]), ("dp", "mp"))
    g_norms = jnp.concatenate([sums, jnp.stack([d_gain1, d_shift1, d_gain2, d_shift2])])
    return (loss, (g_table, g_mixed, g_out, g_inner, g_outer, g_norms))


def on_device(
    token_ids,
    query_lengths,
    negative_mask,
    positive_index,
    used_rows,
    step_count,
    table,
    w_mixed,
    w_out,
    w_inner,
    w_outer,
    norm_params,
    table_m,
    table_v,
    mixed_m,
    mixed_v,
    out_m,
    out_v,
    inner_m,
    inner_v,
    outer_m,
    outer_v,
    norms_m,
    norms_v,
):
    loss, grads = gradients(
        token_ids,
        query_lengths,
        negative_mask,
        positive_index,
        used_rows,
        table,
        w_mixed,
        w_out,
        w_inner,
        w_outer,
        norm_params,
    )
    owner = (lax.axis_index("dp") == 0) & (lax.axis_index("mp") == 0)
    squares = jnp.where(owner, jnp.sum(grads[5] * grads[5]), 0.0)
    for grad in grads[:5]:
        squares = squares + jnp.sum(grad * grad)
    grad_norm = jnp.sqrt(lax.psum(squares, ("enc", "dp", "mp")))
    clip = jnp.minimum(1.0, clip_limit / (grad_norm + 1e-06))
    count = step_count[0].astype(F32)
    masters = (table, w_mixed, w_out, w_inner, w_outer, norm_params)
    firsts = (table_m, mixed_m, out_m, inner_m, outer_m, norms_m)
    seconds = (table_v, mixed_v, out_v, inner_v, outer_v, norms_v)
    results = [loss, grad_norm]
    for index in range(6):
        rate, decay = (0.5, 0.0) if index == 5 else (0.06, 0.01)
        results.extend(
            adam_step(
                masters[index],
                grads[index][None] * clip,
                firsts[index],
                seconds[index],
                rate,
                decay,
                count,
            )
        )
    return tuple(results)


def solution(mesh):
    table = P("enc", ("dp", "mp"), None)
    mixed = P("enc", "dp", None, "mp")
    columns = P("enc", "mp", "dp")
    units = P("enc", "dp", "mp")
    norms = P("enc", None, None)
    matrices = (table, mixed, columns, units, columns, norms)
    moments = tuple((spec for spec in matrices for _ in range(2)))
    updated = tuple((spec for spec in matrices for _ in range(3)))
    return jax.shard_map(
        on_device,
        mesh=mesh,
        in_specs=(P("enc", "dp", None), P("dp"), P(), P(), P(), P()) + matrices + moments,
        out_specs=(P(), P()) + updated,
        check_vma=False,
    )
```

profile of v0, /device:TPU:12, one launch (start us, length us, event | category | flops | bytes accessed | tf_op | source)
XLA Modules:
  0.0 815.6 jit_solution(12494069726686477999)
XLA Ops:
  8.8 3.4 reduce-precision_reduce_fusion
  13.8 13.3 %all-gather = s32[1,16,256]{2,0,1:T(1,128)S(1)} all-gather(s32[1,4,256]{2,0,1:T(1,128)S(1)} %copy.79), channel_id=2, replica_groups=mesh['enc'=2,'dp'=4,'mp'=4] {'dp'}, dimensions={1}, use_global_device_ids=true | all-gather | bytes 20480 | tf_op jit(solution)/shard_map/all_gather | solution.py:105
  27.4 6.3 fusion.4
  33.8 4.5 fusion.5
  40.0 8.2 %all-reduce.1 = s32[32]{0:T(128)S(1)} all-reduce(s32[32]{0:T(128)S(1)} %dynamic-update-slice), channel_id=1, replica_groups=mesh['enc'=2,'dp'=4,'mp'=4] {'dp'}, use_global_device_ids=true, to_apply=%add.1 | all-reduce | flops 32 | bytes 256
  51.7 86.6 %all-reduce.8.cloned.1.call-done = f32[32,768]{1,0:T(8,128)} async-done(((f32[32,768]{1,0:T(8,128)}), f32[32,768]{1,0:T(8,128)}) %all-reduce.8.cloned.1.call-update) | async-done | bytes 98320 | tf_op jit(solution)/shard_map/psum | solution.py:121
  139.3 14.6 %psum.99 = bf16[3,32,64]{2,1,0:T(8,128)(2,1)S(1)} all-reduce(f32[3,32,64]{2,1,0:T(8,128)S(1)} %convolution_bitcast_fusion.1), channel_id=1, replica_groups=mesh['enc'=2,'dp'=4,'mp'=4] {'dp'}, use_global_device_ids=true, to_apply=%region_3.4 | all-reduce | flops 6144 | bytes 36864 | tf_op jit(solution)/shard_map/psum | solution.py:125
  154.6 18.2 %all_gather.41 = bf16[3,32,768]{1,0,2:T(4,128)(2,1)S(1)} all-gather(bf16[3,32,192]{1,0,2:T(4,128)(2,1)S(1)} %copy.83), channel_id=1, replica_groups=mesh['enc'=2,'dp'=4,'mp'=4] {'dp'}, dimensions={2}, use_global_device_ids=true | all-gather | bytes 184320 | tf_op jit(solution)/shard_map/all_gather | solution.py:127
  173.3 10.2 %all_gather.42 = bf16[12,32,768]{2,1,0:T(8,128)(2,1)S(1)} all-gather(bf16[3,32,768]{2,1,0:T(8,128)(2,1)S(1)} %copy.84), channel_id=1, replica_groups=mesh['enc'=2,'dp'=4,'mp'=4] {'mp'}, dimensions={0}, use_global_device_ids=true | all-gather | bytes 737280 | tf_op jit(solution)/shard_map/all_gather | solution.py:127
  184.3 5.8 fusion.135
  190.1 32.9 %pmax.7 = f32[12,32]{1,0:T(8,128)} all-reduce(f32[12,32]{1,0:T(8,128)} %get-tuple-element.83), channel_id=1, replica_groups=mesh['enc'=2,'dp'=4,'mp'=4] {'dp','mp'}, use_global_device_ids=true, to_apply=%region_5.6 | all-reduce | flops 384 | bytes 3072 | tf_op jit(solution)/shard_map/pmax | solution.py:129
  223.1 3.1 fusion.11
  226.1 37.3 %psum.100 = f32[12,32]{1,0:T(8,128)} all-reduce(f32[12,32]{1,0:T(8,128)} %fusion.11), channel_id=1, replica_groups=mesh['enc'=2,'dp'=4,'mp'=4] {'dp','mp'}, use_global_device_ids=true, to_apply=%region_7.8 | all-reduce | flops 384 | bytes 3072 | tf_op jit(solution)/shard_map/psum | solution.py:131
  263.4 4.4 fusion.22
  267.9 36.2 %reduce-scatter.17.cloned.1.call-done = f32[3,32,768]{2,1,0:T(8,128)} async-done(((f32[12,32,768]{2,1,0:T(8,128)}), f32[3,32,768]{2,1,0:T(8,128)}) %reduce-scatter.17.cloned.1.call-update) | async-done | bytes 294928
  311.7 13.1 %reduce-scatter.13.cloned.1.call-done = f32[192,96]{1,0:T(8,128)} async-done(((f32[768,96]{1,0:T(8,128)}), f32[192,96]{1,0:T(8,128)}) %reduce-scatter.13.cloned.1.call-update) | async-done | bytes 73744
  326.1 17.8 %psum.101 = f32[3,32,64]{2,1,0:T(8,128)S(1)} all-reduce(f32[3,32,64]{2,1,0:T(8,128)S(1)} %fusion.141), channel_id=1, replica_groups=mesh['enc'=2,'dp'=4,'mp'=4] {'dp'}, use_global_device_ids=true, to_apply=%region_10.11 | all-reduce | flops 6144 | bytes 49152 | tf_op jit(solution)/shard_map/psum | solution.py:136
  344.1 15.5 %psum.102 = f32[32,192]{1,0:T(8,128)S(1)} all-reduce(f32[32,192]{1,0:T(8,128)S(1)} %convolution_bitcast_fusion.3), channel_id=1, replica_groups=mesh['enc'=2,'dp'=4,'mp'=4] {'mp'}, use_global_device_ids=true, to_apply=%region_11.12 | all-reduce | flops 6144 | bytes 49152 | tf_op jit(solution)/shard_map/psum | solution.py:138
  359.5 13.5 %all-gather.3 = f32[4,192,32]{1,2,0:T(8,128)S(1)} all-gather(f32[1,192,32]{1,2,0:T(8,128)S(1)} %bitcast.263), channel_id=1, replica_groups=mesh['enc'=2,'dp'=4,'mp'=4] {'dp'}, dimensions={0}, use_global_device_ids=true | all-gather | bytes 122880 | tf_op jit(solution)/shard_map/all_gather | solution.py:139
  380.4 30.1 %all-reduce.10.cloned.1.call-done = f32[32,768]{1,0:T(8,128)} async-done(((f32[32,768]{1,0:T(8,128)}), f32[32,768]{1,0:T(8,128)}) %all-reduce.10.cloned.1.call-update) | async-done | bytes 98320 | tf_op jit(solution)/shard_map/psum | solution.py:142
  411.8 15.4 %psum.104 = f32[32,192]{1,0:T(8,128)S(1)} all-reduce(f32[32,192]{1,0:T(8,128)S(1)} %fusion.33), channel_id=1, replica_groups=mesh['enc'=2,'dp'=4,'mp'=4] {'mp'}, use_global_device_ids=true, to_apply=%region_15.16 | all-reduce | flops 6144 | bytes 49152 | tf_op jit(solution)/shard_map/psum | solution.py:145
  427.2 12.2 %all-gather.4 = f32[4,192,32]{1,2,0:T(8,128)S(1)} all-gather(f32[1,192,32]{1,2,0:T(8,128)S(1)} %bitcast.264), channel_id=1, replica_groups=mesh['enc'=2,'dp'=4,'mp'=4] {'dp'}, dimensions={0}, use_global_device_ids=true | all-gather | bytes 122880 | tf_op jit(solution)/shard_map/all_gather | solution.py:146
  441.6 1.9 all-gather.1
  449.2 33.5 %all-reduce.12.cloned.1.call-done = f32[32,768]{1,0:T(8,128)} async-done(((f32[32,768]{1,0:T(8,128)}), f32[32,768]{1,0:T(8,128)}) %all-reduce.12.cloned.1.call-update) | async-done | bytes 98320 | tf_op jit(solution)/shard_map/psum | solution.py:165
  483.9 15.4 %psum.106 = f32[32,192]{1,0:T(8,128)S(1)} all-reduce(f32[32,192]{1,0:T(8,128)S(1)} %fusion.35), channel_id=1, replica_groups=mesh['enc'=2,'dp'=4,'mp'=4] {'mp'}, use_global_device_ids=true, to_apply=%region_32.33 | all-reduce | flops 6144 | bytes 49152 | tf_op jit(solution)/shard_map/psum | solution.py:168
  499.3 12.2 %all-gather.5 = f32[4,192,32]{1,2,0:T(8,128)S(1)} all-gather(f32[1,192,32]{1,2,0:T(8,128)S(1)} %bitcast.265), channel_id=1, replica_groups=mesh['enc'=2,'dp'=4,'mp'=4] {'dp'}, dimensions={0}, use_global_device_ids=true | all-gather | bytes 122880 | tf_op jit(solution)/shard_map/all_gather | solution.py:169
  512.5 16.4 %psum.107 = bf16[3,32,64]{2,1,0:T(8,128)(2,1)S(1)} all-reduce(f32[3,32,64]{2,1,0:T(8,128)S(1)} %convolution_bitcast_fusion), channel_id=1, replica_groups=mesh['enc'=2,'dp'=4,'mp'=4] {'dp'}, use_global_device_ids=true, to_apply=%region_35.36 | all-reduce | flops 6144 | bytes 36864 | tf_op jit(solution)/shard_map/psum | solution.py:173
  529.3 15.9 %all_gather.48 = bf16[3,32,768]{1,0,2:T(4,128)(2,1)S(1)} all-gather(bf16[3,32,192]{1,0,2:T(4,128)(2,1)S(1)} %copy.91), channel_id=1, replica_groups=mesh['enc'=2,'dp'=4,'mp'=4] {'dp'}, dimensions={2}, use_global_device_ids=true | all-gather | bytes 184320 | tf_op jit(solution)/shard_map/all_gather | solution.py:176
  545.6 10.2 %all_gather.49 = bf16[12,32,768]{2,1,0:T(8,128)(2,1)S(1)} all-gather(bf16[3,32,768]{2,1,0:T(8,128)(2,1)S(1)} %copy.92), channel_id=1, replica_groups=mesh['enc'=2,'dp'=4,'mp'=4] {'mp'}, dimensions={0}, use_global_device_ids=true | all-gather | bytes 737280 | tf_op jit(solution)/shard_map/all_gather | solution.py:176
  555.9 7.1 all-gather.6
  563.0 4.3 multiply_convert_fusion
  568.6 2.4 fusion.138
  573.8 2.6 multiply_reduce_fusion.4
  577.5 5.8 fusion.137
  583.4 4.5 fusion.20
  587.9 13.2 %reduce-scatter.19.cloned.1.call-done = f32[3,32,768]{2,1,0:T(8,128)} async-done(((f32[12,32,768]{2,1,0:T(8,128)}), f32[3,32,768]{2,1,0:T(8,128)}) %reduce-scatter.19.cloned.1.call-update) | async-done | bytes 294928
  606.8 1.8 multiply_reduce_fusion.5
  608.7 13.2 %reduce-scatter.15.cloned.1.call-done = f32[192,96]{1,0:T(8,128)} async-done(((f32[768,96]{1,0:T(8,128)}), f32[192,96]{1,0:T(8,128)}) %reduce-scatter.15.cloned.1.call-update) | async-done | bytes 73744
  624.2 17.8 %psum.108 = f32[3,32,64]{2,1,0:T(8,128)S(1)} all-reduce(f32[3,32,64]{2,1,0:T(8,128)S(1)} %fusion.139), channel_id=1, replica_groups=mesh['enc'=2,'dp'=4,'mp'=4] {'dp'}, use_global_device_ids=true, to_apply=%region_39.40 | all-reduce | flops 6144 | bytes 49152 | tf_op jit(solution)/shard_map/psum | solution.py:183
  643.1 15.4 %psum.109 = f32[32,192]{1,0:T(8,128)S(1)} all-reduce(f32[32,192]{1,0:T(8,128)S(1)} %convolution_bitcast_fusion.2), channel_id=1, replica_groups=mesh['enc'=2,'dp'=4,'mp'=4] {'mp'}, use_global_device_ids=true, to_apply=%region_40.41 | all-reduce | flops 6144 | bytes 49152 | tf_op jit(solution)/shard_map/psum | solution.py:188
  658.5 13.3 %all-gather.7 = f32[4,192,32]{1,2,0:T(8,128)S(1)} all-gather(f32[1,192,32]{1,2,0:T(8,128)S(1)} %bitcast.266), channel_id=1, replica_groups=mesh['enc'=2,'dp'=4,'mp'=4] {'dp'}, dimensions={0}, use_global_device_ids=true | all-gather | bytes 122880 | tf_op jit(solution)/shard_map/all_gather | solution.py:189
  672.0 12.5 %multiply_reduce_fusion.1 = (f32[1920]{0:T(1024)S(1)}, f32[768]{0:T(1024)S(1)}, f32[768]{0:T(1024)S(1)}, f32[1920,768]{1,0:T(8,128)}) fusion(f32[768]{0:T(1024)} %copy-done.40, f32[1920]{0:T(1024)S(1)} %broadcast_multiply_fusion.1, f32[1,1920,768]{2,1,0:T(8,128)} %param.30, f32[1920]{0:T(1024)S(1)} %fusion.93, f32[32,768]{1,0:T(8,128)} %copy-done.26, ...), kind=kOutput, calls=%fused_computation.11 | convolution fusion | flops 112173696 | bytes 23821952 | tf_op jit(solution)/shard_map/cv,ci->vi/dot_general | solution.py:27
  684.5 31.3 %psum.110 = f32[2,768]{1,0:T(2,128)S(1)} all-reduce(f32[2,768]{1,0:T(2,128)S(1)} %pad_maximum_fusion), channel_id=1, replica_groups=mesh['enc'=2,'dp'=4,'mp'=4] {'dp','mp'}, use_global_device_ids=true, to_apply=%region_43.44 | all-reduce | flops 1536 | bytes 12288 | tf_op jit(solution)/shard_map/psum | solution.py:196
  716.5 6.1 fusion.126
  722.7 2.5 copy-done.1
  725.2 2.3 multiply_reduce_fusion
  733.2 49.5 %psum.111 = f32[]{:T(128)} all-reduce(f32[]{:T(128)S(6)} %add.308), channel_id=1, replica_groups=mesh['enc'=2,'dp'=4,'mp'=4] {'enc','dp','mp'}, use_global_device_ids=true, to_apply=%region_56.57 | all-reduce | flops 1 | bytes 8 | tf_op jit(solution)/shard_map/psum | solution.py:244
  784.4 15.9 %multiply_subtract_fusion = (f32[1,1920,768]{2,1,0:T(8,128)}, f32[1,1920,768]{2,1,0:T(8,128)}, f32[1,1920,768]{2,1,0:T(8,128)}) fusion(f32[1,1920,768]{2,1,0:T(8,128)} %param.30, f32[]{:T(128)} %bitcast.52, f32[]{:T(128)} %bitcast.50, f32[]{:T(128)S(6)} %min.3, f32[1920,768]{1,0:T(8,128)} %copy-done.1, f32[1920]{0:T(1024)S(1)} %negate_multiply_fusion.1, ...), kind=kLoop, calls=%fused_computation.9 | loop fusion | flops 25067520 | bytes 41295372 | tf_op jit(solution)/shard_map/sub | solution.py:77
  (295 shorter events, 60.9 us)
Async XLA Ops:
  7.2 131.1 %all-reduce.8.cloned.1.call-start = ((), (), s32[]{:S(2)}) async-start(), calls=%async_computation.4 | async-start | bytes 196608 | tf_op jit(solution)/shard_map/psum | solution.py:121
  8.8 25.0 %copy-start.40 = (f32[768]{0:T(1024)}, f32[768]{0:T(1024)S(1)}, u32[]{:S(2)}) copy-start(f32[768]{0:T(1024)S(1)} %get-tuple-element.33) | copy-start | bytes 9220
  27.4 11.0 %copy-start.63 = (s32[32]{0:T(128)}, s32[32]{0:T(128)S(1)}, u32[]{:S(2)}) copy-start(s32[32]{0:T(128)S(1)} %add_subtract_fusion) | copy-start | bytes 388
  33.7 6.0 copy-start.64
  33.8 270.4 %reduce-scatter.17.cloned.1.call-start = ((), (), s32[]{:S(2)}) async-start(), calls=%async_computation.9 | async-start | bytes 1474560
  51.6 102.4 %copy-start.11 = (bf16[1,192,1,192]{1,3,2,0:T(8,128)(2,1)}, bf16[1,192,1,192]{1,3,2,0:T(8,128)(2,1)S(1)}, u32[]{:S(2)}) copy-start(bf16[1,192,1,192]{1,3,2,0:T(8,128)(2,1)S(1)} %copy.82) | copy-start | bytes 221188
  51.7 102.3 %copy-start.10 = (bf16[1,192,1,192]{1,3,2,0:T(8,128)(2,1)}, bf16[1,192,1,192]{1,3,2,0:T(8,128)(2,1)S(1)}, u32[]{:S(2)}) copy-start(bf16[1,192,1,192]{1,3,2,0:T(8,128)(2,1)S(1)} %copy.81) | copy-start | bytes 221188
  183.5 79.9 %copy-start.4 = (bf16[1920,768,1]{1,0,2:T(8,128)(2,1)S(1)}, bf16[1920,768,1]{1,0,2:T(8,128)(2,1)}, u32[]{:S(2)}) copy-start(bf16[1920,768,1]{1,0,2:T(8,128)(2,1)} %fusion.5) | copy-start | bytes 8847364
  267.9 107.4 %copy-start.2 = (f32[1,192,768]{2,1,0:T(8,128)S(1)}, f32[1,192,768]{2,1,0:T(8,128)}, u32[]{:S(2)}) copy-start(f32[1,192,768]{2,1,0:T(8,128)} %param.33) | copy-start | bytes 1769476
  267.9 143.8 %copy-start.3 = (f32[1,768,192]{1,2,0:T(8,128)S(1)}, f32[1,768,192]{1,2,0:T(8,128)}, u32[]{:S(2)}) copy-start(f32[1,768,192]{1,2,0:T(8,128)} %param.34) | copy-start | bytes 1769476
  267.9 56.9 %reduce-scatter.13.cloned.1.call-start = ((), (), s32[]{:S(2)}) async-start(), calls=%async_computation.7 | async-start | bytes 491520
  307.0 204.7 %copy-start.36 = (f32[768]{0:T(1024)S(1)}, f32[768]{0:T(1024)}, u32[]{:S(2)}) copy-start(f32[768]{0:T(1024)} %get-tuple-element.31) | copy-start | bytes 9220
  307.0 103.5 %all-reduce.10.cloned.1.call-start = ((), (), s32[]{:S(2)}) async-start(), calls=%async_computation.5 | async-start | bytes 196608 | tf_op jit(solution)/shard_map/psum | solution.py:142
  325.9 203.2 %copy-start.27 = (bf16[3,32,192]{2,1,0:T(8,128)(2,1)}, bf16[3,32,192]{2,1,0:T(8,128)(2,1)S(1)}, u32[]{:S(2)}) copy-start(bf16[3,32,192]{2,1,0:T(8,128)(2,1)S(1)} %copy.99) | copy-start | bytes 110596
  343.9 201.3 %copy-start.14 = (f32[3,32,64]{2,1,0:T(8,128)}, f32[3,32,64]{2,1,0:T(8,128)S(1)}, u32[]{:S(2)}) copy-start(f32[3,32,64]{2,1,0:T(8,128)S(1)} %psum.101) | copy-start | bytes 73732
  375.3 64.3 %copy-start.34 = (f32[32,768]{1,0:T(8,128)}, f32[32,768]{1,0:T(8,128)S(1)}, u32[]{:S(2)}) copy-start(f32[32,768]{1,0:T(8,128)S(1)} %multiply_add_fusion.4) | copy-start | bytes 294916
  376.2 186.8 %copy-start.9 = (f32[32,1920]{1,0:T(8,128)S(1)}, f32[32,1920]{1,0:T(8,128)}, u32[]{:S(2)}) copy-start(f32[32,1920]{1,0:T(8,128)} %get-tuple-element.75) | copy-start | bytes 737284
  376.2 106.5 %all-reduce.12.cloned.1.call-start = ((), (), s32[]{:S(2)}) async-start(), calls=%async_computation.6 | async-start | bytes 196608 | tf_op jit(solution)/shard_map/psum | solution.py:165
  447.5 64.0 %copy-start.35 = (f32[32,768]{1,0:T(8,128)}, f32[32,768]{1,0:T(8,128)S(1)}, u32[]{:S(2)}) copy-start(f32[32,768]{1,0:T(8,128)S(1)} %broadcast_add_fusion.1) | copy-start | bytes 294916
  448.4 152.7 %reduce-scatter.19.cloned.1.call-start = ((), (), s32[]{:S(2)}) async-start(), calls=%async_computation.10 | async-start | bytes 1474560
  483.7 83.7 %copy-start.29 = (bf16[32,768]{1,0:T(8,128)(2,1)}, bf16[32,768]{1,0:T(8,128)(2,1)S(1)}, u32[]{:S(2)}) copy-start(bf16[32,768]{1,0:T(8,128)(2,1)S(1)} %add_convert_fusion) | copy-start | bytes 147460
  512.0 64.4 %copy-start.48 = (f32[768]{0:T(1024)}, f32[768]{0:T(1024)S(1)}, u32[]{:S(2)}) copy-start(f32[768]{0:T(1024)S(1)} %get-tuple-element.25) | copy-start | bytes 9220
  512.0 64.9 %copy-start.46 = (f32[768]{0:T(1024)}, f32[768]{0:T(1024)S(1)}, u32[]{:S(2)}) copy-start(f32[768]{0:T(1024)S(1)} %get-tuple-element.28) | copy-start | bytes 9220
  512.3 55.1 %copy-start.26 = (f32[32,768]{1,0:T(8,128)}, f32[32,768]{1,0:T(8,128)S(1)}, u32[]{:S(2)}) copy-start(f32[32,768]{1,0:T(8,128)S(1)} %broadcast_add_fusion) | copy-start | bytes 294916
  528.9 38.5 %copy-start.30 = (bf16[3,32,64]{2,1,0:T(8,128)(2,1)}, bf16[3,32,64]{2,1,0:T(8,128)(2,1)S(1)}, u32[]{:S(2)}) copy-start(bf16[3,32,64]{2,1,0:T(8,128)(2,1)S(1)} %psum.107) | copy-start | bytes 36868
  555.9 7.1 copy-start.24
  568.6 8.9 %copy-start.23 = (bf16[12,32,768]{2,1,0:T(8,128)(2,1)S(1)}, bf16[12,32,768]{2,1,0:T(8,128)(2,1)}, u32[]{:S(2)}) copy-start(bf16[12,32,768]{2,1,0:T(8,128)(2,1)} %copy-done.22) | copy-start | bytes 1769476
  571.0 50.9 %reduce-scatter.15.cloned.1.call-start = ((), (), s32[]{:S(2)}) async-start(), calls=%async_computation.8 | async-start | bytes 491520
  577.5 5.9 copy-start.50
  577.5 5.9 copy-start.61
  583.4 20.7 %copy-start.28 = (bf16[3,32,192]{2,1,0:T(8,128)(2,1)S(1)}, bf16[3,32,192]{2,1,0:T(8,128)(2,1)}, u32[]{:S(2)}) copy-start(bf16[3,32,192]{2,1,0:T(8,128)(2,1)} %copy-done.27) | copy-start | bytes 110596
  583.4 21.8 %copy-start.15 = (f32[3,32,64]{2,1,0:T(8,128)S(1)}, f32[3,32,64]{2,1,0:T(8,128)}, u32[]{:S(2)}) copy-start(f32[3,32,64]{2,1,0:T(8,128)} %copy-done.14) | copy-start | bytes 73732
  587.9 35.1 %copy-start.12 = (bf16[1,192,1,192]{1,3,2,0:T(8,128)(2,1)S(1)}, bf16[1,192,1,192]{1,3,2,0:T(8,128)(2,1)}, u32[]{:S(2)}) copy-start(bf16[1,192,1,192]{1,3,2,0:T(8,128)(2,1)} %copy-done.11) | copy-start | bytes 221188
  671.9 43.9 %copy-start.57 = (f32[1,768]{1,0:T(1,128)S(1)}, f32[1,768]{1,0:T(1,128)}, u32[]{:S(2)}) copy-start(f32[1,768]{1,0:T(1,128)} %reshape.653) | copy-start | bytes 9220
  672.0 43.9 %copy-start.58 = (f32[1,768]{1,0:T(1,128)S(1)}, f32[1,768]{1,0:T(1,128)}, u32[]{:S(2)}) copy-start(f32[1,768]{1,0:T(1,128)} %reshape.654) | copy-start | bytes 9220
  672.0 43.9 %copy-start.59 = (f32[1,768]{1,0:T(1,128)S(1)}, f32[1,768]{1,0:T(1,128)}, u32[]{:S(2)}) copy-start(f32[1,768]{1,0:T(1,128)} %reshape.651) | copy-start | bytes 9220
  672.0 43.9 %copy-start.60 = (f32[1,768]{1,0:T(1,128)S(1)}, f32[1,768]{1,0:T(1,128)}, u32[]{:S(2)}) copy-start(f32[1,768]{1,0:T(1,128)} %reshape.652) | copy-start | bytes 9220
  672.0 44.5 %copy-start.38 = (f32[1920]{0:T(1024)S(1)}, f32[1920]{0:T(1024)}, u32[]{:S(2)}) copy-start(f32[1920]{0:T(1024)} %copy-done.37) | copy-start | bytes 23044
  672.0 44.5 %copy-start.41 = (f32[768]{0:T(1024)S(1)}, f32[768]{0:T(1024)}, u32[]{:S(2)}) copy-start(f32[768]{0:T(1024)} %copy-done.40) | copy-start | bytes 9220
  722.7 60.9 %copy-start.49 = (f32[768]{0:T(1024)S(1)}, f32[768]{0:T(1024)}, u32[]{:S(2)}) copy-start(f32[768]{0:T(1024)} %copy-done.48) | copy-start | bytes 9220
  722.7 61.0 %copy-start.47 = (f32[768]{0:T(1024)S(1)}, f32[768]{0:T(1024)}, u32[]{:S(2)}) copy-start(f32[768]{0:T(1024)} %copy-done.46) | copy-start | bytes 9220
  722.7 61.0 %copy-start.45 = (f32[768]{0:T(1024)S(1)}, f32[768]{0:T(1024)}, u32[]{:S(2)}) copy-start(f32[768]{0:T(1024)} %get-tuple-element.23) | copy-start | bytes 9220
  722.7 61.0 %copy-start.43 = (f32[768]{0:T(1024)S(1)}, f32[768]{0:T(1024)}, u32[]{:S(2)}) copy-start(f32[768]{0:T(1024)} %get-tuple-element.27) | copy-start | bytes 9220
  784.3 16.1 %copy-start.13 = (f32[1,192,192]{2,1,0:T(8,128)S(1)}, f32[1,192,192]{2,1,0:T(8,128)}, u32[]{:S(2)}) copy-start(f32[1,192,192]{2,1,0:T(8,128)} %param.32) | copy-start | bytes 442372
  784.3 16.1 %copy-start.32 = (f32[1,192,192]{2,1,0:T(8,128)S(1)}, f32[1,192,192]{2,1,0:T(8,128)}, u32[]{:S(2)}) copy-start(f32[1,192,192]{2,1,0:T(8,128)} %param.41) | copy-start | bytes 442372
  784.4 16.0 %copy-start.33 = (f32[1,192,192]{2,1,0:T(8,128)S(1)}, f32[1,192,192]{2,1,0:T(8,128)}, u32[]{:S(2)}) copy-start(f32[1,192,192]{2,1,0:T(8,128)} %param.40) | copy-start | bytes 442372
  784.4 16.9 %copy-start.16 = (f32[1,192,768]{2,1,0:T(8,128)S(1)}, f32[1,192,768]{2,1,0:T(8,128)}, u32[]{:S(2)}) copy-start(f32[1,192,768]{2,1,0:T(8,128)} %param.43) | copy-start | bytes 1769476
  784.4 16.9 %copy-start.17 = (f32[1,192,768]{2,1,0:T(8,128)S(1)}, f32[1,192,768]{2,1,0:T(8,128)}, u32[]{:S(2)}) copy-start(f32[1,192,768]{2,1,0:T(8,128)} %param.42) | copy-start | bytes 1769476
  (26 other events, 89.7 us)
Sparse Core Ops, SparseCore 0:
  33.9 104.3 all-reduce.7
  268.0 36.0 reduce-scatter.16
  307.2 17.5 reduce-scatter.12
  376.3 34.1 all-reduce.9
  448.5 34.1 all-reduce.11
  571.1 29.9 reduce-scatter.18
  604.2 17.6 reduce-scatter.14
where the time goes:
time: 817 us; the launch traced here: 816 us
  blocking collectives  416 us (51%)
  waiting for transfers between devices  226 us (28%)
  matrix products  62.6 us (8%)
  other arithmetic  59.2 us (7%)
  local copies, waits for them, and re-layouts  26.8 us (3%)
  between operations  24.9 us (3%)
    psum x1, waiting for transfers between devices, gradients(): lax.psum(jnp.dot(cls_hot.astype(F32), hidden, precision=exact_arithmetic_...  86.6 us
    unnamed x11, waiting for transfers between devices  75.8 us
    dot_general x26, matrix products, mul(): return jnp.einsum(spec, a, b, preferred_element_type=F32)  55.2 us
    psum x1, blocking collectives, on_device(): grad_norm = jnp.sqrt(lax.psum(squares, ('enc', 'dp', 'mp')))  49.5 us
    psum x1, blocking collectives, gradients(): probs = weight / lax.psum(jnp.sum(weight, -1, keepdims=True), ('dp', 'mp'))  37.3 us
    psum x1, waiting for transfers between devices, gradients(): d_act = lax.psum(mul('ce,fe->cf', d_outer, wt), 'dp')  33.5 us
    pmax x1, blocking collectives, gradients(): top = lax.pmax(jnp.max(scores, -1, keepdims=True), ('dp', 'mp'))  32.9 us
    psum x1, blocking collectives, gradients(): sums = lax.psum(jnp.stack([d_gain0, d_shift0]), ('dp', 'mp'))  31.3 us
  transfers between devices with their start and end apart: 7, of which 7 were waited for; matrix products, arithmetic and copies ran while one was open for 5% of the time, Pallas kernels for 0%

commit v1 on v0

--- a/solution.py
+++ b/solution.py
@@ -119,7 +119,7 @@
     hidden, hidden_back = jax.vjp(layer_norm, embedded, norms[0], norms[1])
     hid = hidden.astype(BF16)
     first_rows = lax.psum(
-        jnp.dot(cls_hot.astype(F32), hidden, precision=exact_arithmetic_level), ("dp", "mp")
+        lax.psum(jnp.dot(cls_hot.astype(F32), hidden, precision=exact_arithmetic_level), "mp"), "dp"
     )
     first_mine = mine(first_rows).astype(BF16)
     q = lax.psum(mul("ci,ihk->hck", first_mine, wq), "dp").astype(BF16)

time: 817 us -> 792 us (0.969)
  waiting for transfers between devices: 226 us -> 201 us
    psum x1, waiting for transfers between devices: 86.6 us -> 25.7 us  [gradients(): lax.psum(jnp.dot(cls_hot.astype(F32), hidden, precision=exact_arithmetic_...]
    psum x0 -> x1, waiting for transfers between devices: none -> 35.7 us  [gradients(): lax.psum(lax.psum(jnp.dot(cls_hot.astype(F32), hidden, precision=exact_ar...]
    unnamed x11 -> x12, waiting for transfers between devices: 75.8 us -> 75.6 us
  transfers between devices with their start and end apart: 7 -> 8, of which waited for: 7 -> 8; matrix products, arithmetic and copies ran while one was open for 5% -> 5% of each run, Pallas kernels for 0% -> 0%
where the time goes in v1:
time: 792 us; the launch traced here: 791 us
  blocking collectives  416 us (53%)
  waiting for transfers between devices  201 us (25%)
  matrix products  62.6 us (8%)
  other arithmetic  59.3 us (7%)
  local copies, waits for them, and re-layouts  26.8 us (3%)
  between operations  24.9 us (3%)
    unnamed x12, waiting for transfers between devices  75.6 us
    dot_general x26, matrix products, mul(): return jnp.einsum(spec, a, b, preferred_element_type=F32)  55.2 us
    psum x1, blocking collectives, on_device(): grad_norm = jnp.sqrt(lax.psum(squares, ('enc', 'dp', 'mp')))  49.4 us
    psum x1, blocking collectives, gradients(): probs = weight / lax.psum(jnp.sum(weight, -1, keepdims=True), ('dp', 'mp'))  37.4 us
    psum x1, waiting for transfers between devices, gradients(): lax.psum(lax.psum(jnp.dot(cls_hot.astype(F32), hidden, precision=exact_ar...  35.7 us
    psum x1, waiting for transfers between devices, gradients(): d_act = lax.psum(mul('ce,fe->cf', d_outer, wt), 'dp')  33.5 us
    pmax x1, blocking collectives, gradients(): top = lax.pmax(jnp.max(scores, -1, keepdims=True), ('dp', 'mp'))  33.3 us
    psum x1, blocking collectives, gradients(): sums = lax.psum(jnp.stack([d_gain0, d_shift0]), ('dp', 'mp'))  31.2 us
  transfers between devices with their start and end apart: 8, of which 8 were waited for; matrix products, arithmetic and copies ran while one was open for 5% of the time, Pallas kernels for 0%

profile of v1, /device:TPU:12, one launch (start us, length us, event | category | flops | bytes accessed | tf_op | source)
XLA Modules:
  0.0 790.5 jit_solution(5123507282730193173)
XLA Ops:
  8.8 3.4 reduce-precision_reduce_fusion
  13.8 13.3 %all-gather = s32[1,16,256]{2,0,1:T(1,128)S(1)} all-gather(s32[1,4,256]{2,0,1:T(1,128)S(1)} %copy.79), channel_id=2, replica_groups=mesh['enc'=2,'dp'=4,'mp'=4] {'dp'}, dimensions={1}, use_global_device_ids=true | all-gather | bytes 20480 | tf_op jit(solution)/shard_map/all_gather | solution.py:105
  27.4 6.3 fusion.4
  33.8 4.6 fusion.5
  40.0 8.2 %all-reduce.1 = s32[32]{0:T(128)S(1)} all-reduce(s32[32]{0:T(128)S(1)} %dynamic-update-slice), channel_id=1, replica_groups=mesh['enc'=2,'dp'=4,'mp'=4] {'dp'}, use_global_device_ids=true, to_apply=%add.1 | all-reduce | flops 32 | bytes 256
  50.9 25.7 %all-reduce.9.cloned.1.call-done = f32[32,768]{1,0:T(8,128)} async-done(((f32[32,768]{1,0:T(8,128)}), f32[32,768]{1,0:T(8,128)}) %all-reduce.9.cloned.1.call-update) | async-done | bytes 98320 | tf_op jit(solution)/shard_map/psum | solution.py:122
  77.6 35.7 %all-reduce.11.cloned.1.call-done = f32[32,768]{1,0:T(8,128)} async-done(((f32[32,768]{1,0:T(8,128)}), f32[32,768]{1,0:T(8,128)}) %all-reduce.11.cloned.1.call-update) | async-done | bytes 98320 | tf_op jit(solution)/shard_map/psum | solution.py:121
  114.2 14.9 %psum.107 = bf16[3,32,64]{2,1,0:T(8,128)(2,1)S(1)} all-reduce(f32[3,32,64]{2,1,0:T(8,128)S(1)} %convolution_bitcast_fusion.1), channel_id=1, replica_groups=mesh['enc'=2,'dp'=4,'mp'=4] {'dp'}, use_global_device_ids=true, to_apply=%region_4.5 | all-reduce | flops 6144 | bytes 36864 | tf_op jit(solution)/shard_map/psum | solution.py:125
  129.9 17.8 %all_gather.41 = bf16[3,32,768]{1,0,2:T(4,128)(2,1)S(1)} all-gather(bf16[3,32,192]{1,0,2:T(4,128)(2,1)S(1)} %copy.83), channel_id=1, replica_groups=mesh['enc'=2,'dp'=4,'mp'=4] {'dp'}, dimensions={2}, use_global_device_ids=true | all-gather | bytes 184320 | tf_op jit(solution)/shard_map/all_gather | solution.py:127
  148.1 10.3 %all_gather.42 = bf16[12,32,768]{2,1,0:T(8,128)(2,1)S(1)} all-gather(bf16[3,32,768]{2,1,0:T(8,128)(2,1)S(1)} %copy.84), channel_id=1, replica_groups=mesh['enc'=2,'dp'=4,'mp'=4] {'mp'}, dimensions={0}, use_global_device_ids=true | all-gather | bytes 737280 | tf_op jit(solution)/shard_map/all_gather | solution.py:127
  159.2 5.8 fusion.135
  165.0 33.3 %pmax.7 = f32[12,32]{1,0:T(8,128)} all-reduce(f32[12,32]{1,0:T(8,128)} %get-tuple-element.83), channel_id=1, replica_groups=mesh['enc'=2,'dp'=4,'mp'=4] {'dp','mp'}, use_global_device_ids=true, to_apply=%region_6.7 | all-reduce | flops 384 | bytes 3072 | tf_op jit(solution)/shard_map/pmax | solution.py:129
  198.2 3.1 fusion.11
  201.3 37.4 %psum.108 = f32[12,32]{1,0:T(8,128)} all-reduce(f32[12,32]{1,0:T(8,128)} %fusion.11), channel_id=1, replica_groups=mesh['enc'=2,'dp'=4,'mp'=4] {'dp','mp'}, use_global_device_ids=true, to_apply=%region_8.9 | all-reduce | flops 384 | bytes 3072 | tf_op jit(solution)/shard_map/psum | solution.py:131
  238.7 4.4 fusion.22
  243.2 35.9 %reduce-scatter.17.cloned.1.call-done = f32[3,32,768]{2,1,0:T(8,128)} async-done(((f32[12,32,768]{2,1,0:T(8,128)}), f32[3,32,768]{2,1,0:T(8,128)}) %reduce-scatter.17.cloned.1.call-update) | async-done | bytes 294928
  286.6 13.1 %reduce-scatter.13.cloned.1.call-done = f32[192,96]{1,0:T(8,128)} async-done(((f32[768,96]{1,0:T(8,128)}), f32[192,96]{1,0:T(8,128)}) %reduce-scatter.13.cloned.1.call-update) | async-done | bytes 73744
  301.0 17.8 %psum.109 = f32[3,32,64]{2,1,0:T(8,128)S(1)} all-reduce(f32[3,32,64]{2,1,0:T(8,128)S(1)} %fusion.141), channel_id=1, replica_groups=mesh['enc'=2,'dp'=4,'mp'=4] {'dp'}, use_global_device_ids=true, to_apply=%region_11.12 | all-reduce | flops 6144 | bytes 49152 | tf_op jit(solution)/shard_map/psum | solution.py:136
  319.0 15.4 %psum.110 = f32[32,192]{1,0:T(8,128)S(1)} all-reduce(f32[32,192]{1,0:T(8,128)S(1)} %convolution_bitcast_fusion.3), channel_id=1, replica_groups=mesh['enc'=2,'dp'=4,'mp'=4] {'mp'}, use_global_device_ids=true, to_apply=%region_12.13 | all-reduce | flops 6144 | bytes 49152 | tf_op jit(solution)/shard_map/psum | solution.py:138
  334.5 13.5 %all-gather.3 = f32[4,192,32]{1,2,0:T(8,128)S(1)} all-gather(f32[1,192,32]{1,2,0:T(8,128)S(1)} %bitcast.263), channel_id=1, replica_groups=mesh['enc'=2,'dp'=4,'mp'=4] {'dp'}, dimensions={0}, use_global_device_ids=true | all-gather | bytes 122880 | tf_op jit(solution)/shard_map/all_gather | solution.py:139
  355.4 30.1 %all-reduce.13.cloned.1.call-done = f32[32,768]{1,0:T(8,128)} async-done(((f32[32,768]{1,0:T(8,128)}), f32[32,768]{1,0:T(8,128)}) %all-reduce.13.cloned.1.call-update) | async-done | bytes 98320 | tf_op jit(solution)/shard_map/psum | solution.py:142
  386.7 15.4 %psum.112 = f32[32,192]{1,0:T(8,128)S(1)} all-reduce(f32[32,192]{1,0:T(8,128)S(1)} %fusion.33), channel_id=1, replica_groups=mesh['enc'=2,'dp'=4,'mp'=4] {'mp'}, use_global_device_ids=true, to_apply=%region_16.17 | all-reduce | flops 6144 | bytes 49152 | tf_op jit(solution)/shard_map/psum | solution.py:145
  402.2 12.2 %all-gather.4 = f32[4,192,32]{1,2,0:T(8,128)S(1)} all-gather(f32[1,192,32]{1,2,0:T(8,128)S(1)} %bitcast.264), channel_id=1, replica_groups=mesh['enc'=2,'dp'=4,'mp'=4] {'dp'}, dimensions={0}, use_global_device_ids=true | all-gather | bytes 122880 | tf_op jit(solution)/shard_map/all_gather | solution.py:146
  416.5 1.9 all-gather.1
  424.1 33.5 %all-reduce.15.cloned.1.call-done = f32[32,768]{1,0:T(8,128)} async-done(((f32[32,768]{1,0:T(8,128)}), f32[32,768]{1,0:T(8,128)}) %all-reduce.15.cloned.1.call-update) | async-done | bytes 98320 | tf_op jit(solution)/shard_map/psum | solution.py:165
  458.8 15.4 %psum.114 = f32[32,192]{1,0:T(8,128)S(1)} all-reduce(f32[32,192]{1,0:T(8,128)S(1)} %fusion.35), channel_id=1, replica_groups=mesh['enc'=2,'dp'=4,'mp'=4] {'mp'}, use_global_device_ids=true, to_apply=%region_33.34 | all-reduce | flops 6144 | bytes 49152 | tf_op jit(solution)/shard_map/psum | solution.py:168
  474.2 12.2 %all-gather.5 = f32[4,192,32]{1,2,0:T(8,128)S(1)} all-gather(f32[1,192,32]{1,2,0:T(8,128)S(1)} %bitcast.265), channel_id=1, replica_groups=mesh['enc'=2,'dp'=4,'mp'=4] {'dp'}, dimensions={0}, use_global_device_ids=true | all-gather | bytes 122880 | tf_op jit(solution)/shard_map/all_gather | solution.py:169
  487.4 16.4 %psum.115 = bf16[3,32,64]{2,1,0:T(8,128)(2,1)S(1)} all-reduce(f32[3,32,64]{2,1,0:T(8,128)S(1)} %convolution_bitcast_fusion), channel_id=1, replica_groups=mesh['enc'=2,'dp'=4,'mp'=4] {'dp'}, use_global_device_ids=true, to_apply=%region_36.37 | all-reduce | flops 6144 | bytes 36864 | tf_op jit(solution)/shard_map/psum | solution.py:173
  504.2 15.9 %all_gather.48 = bf16[3,32,768]{1,0,2:T(4,128)(2,1)S(1)} all-gather(bf16[3,32,192]{1,0,2:T(4,128)(2,1)S(1)} %copy.91), channel_id=1, replica_groups=mesh['enc'=2,'dp'=4,'mp'=4] {'dp'}, dimensions={2}, use_global_device_ids=true | all-gather | bytes 184320 | tf_op jit(solution)/shard_map/all_gather | solution.py:176
  520.5 10.2 %all_gather.49 = bf16[12,32,768]{2,1,0:T(8,128)(2,1)S(1)} all-gather(bf16[3,32,768]{2,1,0:T(8,128)(2,1)S(1)} %copy.92), channel_id=1, replica_groups=mesh['enc'=2,'dp'=4,'mp'=4] {'mp'}, dimensions={0}, use_global_device_ids=true | all-gather | bytes 737280 | tf_op jit(solution)/shard_map/all_gather | solution.py:176
  530.8 7.1 all-gather.6
  537.9 4.3 multiply_convert_fusion
  543.5 2.4 fusion.138
  548.7 2.6 multiply_reduce_fusion.4
  552.4 5.8 fusion.137
  558.3 4.5 fusion.20
  562.8 13.3 %reduce-scatter.19.cloned.1.call-done = f32[3,32,768]{2,1,0:T(8,128)} async-done(((f32[12,32,768]{2,1,0:T(8,128)}), f32[3,32,768]{2,1,0:T(8,128)}) %reduce-scatter.19.cloned.1.call-update) | async-done | bytes 294928
  583.6 13.2 %reduce-scatter.15.cloned.1.call-done = f32[192,96]{1,0:T(8,128)} async-done(((f32[768,96]{1,0:T(8,128)}), f32[192,96]{1,0:T(8,128)}) %reduce-scatter.15.cloned.1.call-update) | async-done | bytes 73744
  599.2 17.8 %psum.116 = f32[3,32,64]{2,1,0:T(8,128)S(1)} all-reduce(f32[3,32,64]{2,1,0:T(8,128)S(1)} %fusion.139), channel_id=1, replica_groups=mesh['enc'=2,'dp'=4,'mp'=4] {'dp'}, use_global_device_ids=true, to_apply=%region_40.41 | all-reduce | flops 6144 | bytes 49152 | tf_op jit(solution)/shard_map/psum | solution.py:183
  618.0 15.4 %psum.117 = f32[32,192]{1,0:T(8,128)S(1)} all-reduce(f32[32,192]{1,0:T(8,128)S(1)} %convolution_bitcast_fusion.2), channel_id=1, replica_groups=mesh['enc'=2,'dp'=4,'mp'=4] {'mp'}, use_global_device_ids=true, to_apply=%region_41.42 | all-reduce | flops 6144 | bytes 49152 | tf_op jit(solution)/shard_map/psum | solution.py:188
  633.4 13.3 %all-gather.7 = f32[4,192,32]{1,2,0:T(8,128)S(1)} all-gather(f32[1,192,32]{1,2,0:T(8,128)S(1)} %bitcast.266), channel_id=1, replica_groups=mesh['enc'=2,'dp'=4,'mp'=4] {'dp'}, dimensions={0}, use_global_device_ids=true | all-gather | bytes 122880 | tf_op jit(solution)/shard_map/all_gather | solution.py:189
  647.0 12.5 %multiply_reduce_fusion.1 = (f32[1920]{0:T(1024)S(1)}, f32[768]{0:T(1024)S(1)}, f32[768]{0:T(1024)S(1)}, f32[1920,768]{1,0:T(8,128)}) fusion(f32[768]{0:T(1024)} %copy-done.40, f32[1920]{0:T(1024)S(1)} %broadcast_multiply_fusion.1, f32[1,1920,768]{2,1,0:T(8,128)} %param.30, f32[1920]{0:T(1024)S(1)} %fusion.93, f32[32,768]{1,0:T(8,128)} %copy-done.26, ...), kind=kOutput, calls=%fused_computation.11 | convolution fusion | flops 112173696 | bytes 23821952 | tf_op jit(solution)/shard_map/cv,ci->vi/dot_general | solution.py:27
  659.5 31.2 %psum.118 = f32[2,768]{1,0:T(2,128)S(1)} all-reduce(f32[2,768]{1,0:T(2,128)S(1)} %pad_maximum_fusion), channel_id=1, replica_groups=mesh['enc'=2,'dp'=4,'mp'=4] {'dp','mp'}, use_global_device_ids=true, to_apply=%region_44.45 | all-reduce | flops 1536 | bytes 12288 | tf_op jit(solution)/shard_map/psum | solution.py:196
  691.4 6.1 fusion.126
  697.6 2.5 copy-done.1
  700.1 2.3 multiply_reduce_fusion
  708.1 49.4 %psum.119 = f32[]{:T(128)} all-reduce(f32[]{:T(128)S(6)} %add.310), channel_id=1, replica_groups=mesh['enc'=2,'dp'=4,'mp'=4] {'enc','dp','mp'}, use_global_device_ids=true, to_apply=%region_57.58 | all-reduce | flops 1 | bytes 8 | tf_op jit(solution)/shard_map/psum | solution.py:244
  759.3 15.9 %multiply_subtract_fusion = (f32[1,1920,768]{2,1,0:T(8,128)}, f32[1,1920,768]{2,1,0:T(8,128)}, f32[1,1920,768]{2,1,0:T(8,128)}) fusion(f32[1,1920,768]{2,1,0:T(8,128)} %param.30, f32[]{:T(128)} %bitcast.52, f32[]{:T(128)} %bitcast.50, f32[]{:T(128)S(6)} %min.3, f32[1920,768]{1,0:T(8,128)} %copy-done.1, f32[1920]{0:T(1024)S(1)} %negate_multiply_fusion.1, ...), kind=kLoop, calls=%fused_computation.9 | loop fusion | flops 25067520 | bytes 41295372 | tf_op jit(solution)/shard_map/sub | solution.py:77
  (298 shorter events, 62.8 us)
Async XLA Ops:
  7.2 69.4 %all-reduce.9.cloned.1.call-start = ((), (), s32[]{:S(2)}) async-start(), calls=%async_computation.4 | async-start | bytes 196608 | tf_op jit(solution)/shard_map/psum | solution.py:122
  8.8 25.0 %copy-start.40 = (f32[768]{0:T(1024)}, f32[768]{0:T(1024)S(1)}, u32[]{:S(2)}) copy-start(f32[768]{0:T(1024)S(1)} %get-tuple-element.33) | copy-start | bytes 9220
  27.4 6.4 copy-start.63
  33.7 6.0 copy-start.64
  33.7 17.1 %copy-start.7 = (f32[1,192,3,192]{3,1,2,0:T(8,128)S(1)}, f32[1,192,3,192]{3,1,2,0:T(8,128)}, u32[]{:S(2)}) copy-start(f32[1,192,3,192]{3,1,2,0:T(8,128)} %param.31) | copy-start | bytes 1327108
  33.8 79.5 %all-reduce.11.cloned.1.call-start = ((), (), s32[]{:S(2)}) async-start(), calls=%async_computation.5 | async-start | bytes 196608 | tf_op jit(solution)/shard_map/psum | solution.py:121
  76.6 202.5 %reduce-scatter.17.cloned.1.call-start = ((), (), s32[]{:S(2)}) async-start(), calls=%async_computation.10 | async-start | bytes 1474560
  77.4 51.8 %copy-start.11 = (bf16[1,192,1,192]{1,3,2,0:T(8,128)(2,1)}, bf16[1,192,1,192]{1,3,2,0:T(8,128)(2,1)S(1)}, u32[]{:S(2)}) copy-start(bf16[1,192,1,192]{1,3,2,0:T(8,128)(2,1)S(1)} %copy.82) | copy-start | bytes 221188
  77.5 51.7 %copy-start.10 = (bf16[1,192,1,192]{1,3,2,0:T(8,128)(2,1)}, bf16[1,192,1,192]{1,3,2,0:T(8,128)(2,1)S(1)}, u32[]{:S(2)}) copy-start(bf16[1,192,1,192]{1,3,2,0:T(8,128)(2,1)S(1)} %copy.81) | copy-start | bytes 221188
  158.4 80.3 %copy-start.4 = (bf16[1920,768,1]{1,0,2:T(8,128)(2,1)S(1)}, bf16[1920,768,1]{1,0,2:T(8,128)(2,1)}, u32[]{:S(2)}) copy-start(bf16[1920,768,1]{1,0,2:T(8,128)(2,1)} %fusion.5) | copy-start | bytes 8847364
  243.1 107.1 %copy-start.2 = (f32[1,192,768]{2,1,0:T(8,128)S(1)}, f32[1,192,768]{2,1,0:T(8,128)}, u32[]{:S(2)}) copy-start(f32[1,192,768]{2,1,0:T(8,128)} %param.33) | copy-start | bytes 1769476
  243.1 143.4 %copy-start.3 = (f32[1,768,192]{1,2,0:T(8,128)S(1)}, f32[1,768,192]{1,2,0:T(8,128)}, u32[]{:S(2)}) copy-start(f32[1,768,192]{1,2,0:T(8,128)} %param.34) | copy-start | bytes 1769476
  243.1 56.6 %reduce-scatter.13.cloned.1.call-start = ((), (), s32[]{:S(2)}) async-start(), calls=%async_computation.8 | async-start | bytes 491520
  282.0 204.7 %copy-start.36 = (f32[768]{0:T(1024)S(1)}, f32[768]{0:T(1024)}, u32[]{:S(2)}) copy-start(f32[768]{0:T(1024)} %get-tuple-element.31) | copy-start | bytes 9220
  282.0 103.5 %all-reduce.13.cloned.1.call-start = ((), (), s32[]{:S(2)}) async-start(), calls=%async_computation.6 | async-start | bytes 196608 | tf_op jit(solution)/shard_map/psum | solution.py:142
  300.9 203.1 %copy-start.27 = (bf16[3,32,192]{2,1,0:T(8,128)(2,1)}, bf16[3,32,192]{2,1,0:T(8,128)(2,1)S(1)}, u32[]{:S(2)}) copy-start(bf16[3,32,192]{2,1,0:T(8,128)(2,1)S(1)} %copy.99) | copy-start | bytes 110596
  318.8 201.2 %copy-start.14 = (f32[3,32,64]{2,1,0:T(8,128)}, f32[3,32,64]{2,1,0:T(8,128)S(1)}, u32[]{:S(2)}) copy-start(f32[3,32,64]{2,1,0:T(8,128)S(1)} %psum.109) | copy-start | bytes 73732
  350.2 64.3 %copy-start.34 = (f32[32,768]{1,0:T(8,128)}, f32[32,768]{1,0:T(8,128)S(1)}, u32[]{:S(2)}) copy-start(f32[32,768]{1,0:T(8,128)S(1)} %multiply_add_fusion.4) | copy-start | bytes 294916
  351.1 186.8 %copy-start.9 = (f32[32,1920]{1,0:T(8,128)S(1)}, f32[32,1920]{1,0:T(8,128)}, u32[]{:S(2)}) copy-start(f32[32,1920]{1,0:T(8,128)} %get-tuple-element.75) | copy-start | bytes 737284
  351.1 106.5 %all-reduce.15.cloned.1.call-start = ((), (), s32[]{:S(2)}) async-start(), calls=%async_computation.7 | async-start | bytes 196608 | tf_op jit(solution)/shard_map/psum | solution.py:165
  422.4 64.0 %copy-start.35 = (f32[32,768]{1,0:T(8,128)}, f32[32,768]{1,0:T(8,128)S(1)}, u32[]{:S(2)}) copy-start(f32[32,768]{1,0:T(8,128)S(1)} %broadcast_add_fusion.1) | copy-start | bytes 294916
  423.3 152.8 %reduce-scatter.19.cloned.1.call-start = ((), (), s32[]{:S(2)}) async-start(), calls=%async_computation.11 | async-start | bytes 1474560
  458.6 83.7 %copy-start.29 = (bf16[32,768]{1,0:T(8,128)(2,1)}, bf16[32,768]{1,0:T(8,128)(2,1)S(1)}, u32[]{:S(2)}) copy-start(bf16[32,768]{1,0:T(8,128)(2,1)S(1)} %add_convert_fusion) | copy-start | bytes 147460
  486.9 64.4 %copy-start.48 = (f32[768]{0:T(1024)}, f32[768]{0:T(1024)S(1)}, u32[]{:S(2)}) copy-start(f32[768]{0:T(1024)S(1)} %get-tuple-element.25) | copy-start | bytes 9220
  486.9 64.9 %copy-start.46 = (f32[768]{0:T(1024)}, f32[768]{0:T(1024)S(1)}, u32[]{:S(2)}) copy-start(f32[768]{0:T(1024)S(1)} %get-tuple-element.28) | copy-start | bytes 9220
  487.2 55.1 %copy-start.26 = (f32[32,768]{1,0:T(8,128)}, f32[32,768]{1,0:T(8,128)S(1)}, u32[]{:S(2)}) copy-start(f32[32,768]{1,0:T(8,128)S(1)} %broadcast_add_fusion) | copy-start | bytes 294916
  503.8 38.5 %copy-start.30 = (bf16[3,32,64]{2,1,0:T(8,128)(2,1)}, bf16[3,32,64]{2,1,0:T(8,128)(2,1)S(1)}, u32[]{:S(2)}) copy-start(bf16[3,32,64]{2,1,0:T(8,128)(2,1)S(1)} %psum.115) | copy-start | bytes 36868
  530.8 7.1 copy-start.24
  543.5 8.9 %copy-start.23 = (bf16[12,32,768]{2,1,0:T(8,128)(2,1)S(1)}, bf16[12,32,768]{2,1,0:T(8,128)(2,1)}, u32[]{:S(2)}) copy-start(bf16[12,32,768]{2,1,0:T(8,128)(2,1)} %copy-done.22) | copy-start | bytes 1769476
  545.9 50.9 %reduce-scatter.15.cloned.1.call-start = ((), (), s32[]{:S(2)}) async-start(), calls=%async_computation.9 | async-start | bytes 491520
  558.3 20.7 %copy-start.28 = (bf16[3,32,192]{2,1,0:T(8,128)(2,1)S(1)}, bf16[3,32,192]{2,1,0:T(8,128)(2,1)}, u32[]{:S(2)}) copy-start(bf16[3,32,192]{2,1,0:T(8,128)(2,1)} %copy-done.27) | copy-start | bytes 110596
  558.3 21.8 %copy-start.15 = (f32[3,32,64]{2,1,0:T(8,128)S(1)}, f32[3,32,64]{2,1,0:T(8,128)}, u32[]{:S(2)}) copy-start(f32[3,32,64]{2,1,0:T(8,128)} %copy-done.14) | copy-start | bytes 73732
  562.8 35.2 %copy-start.12 = (bf16[1,192,1,192]{1,3,2,0:T(8,128)(2,1)S(1)}, bf16[1,192,1,192]{1,3,2,0:T(8,128)(2,1)}, u32[]{:S(2)}) copy-start(bf16[1,192,1,192]{1,3,2,0:T(8,128)(2,1)} %copy-done.11) | copy-start | bytes 221188
  646.9 43.8 %copy-start.57 = (f32[1,768]{1,0:T(1,128)S(1)}, f32[1,768]{1,0:T(1,128)}, u32[]{:S(2)}) copy-start(f32[1,768]{1,0:T(1,128)} %reshape.653) | copy-start | bytes 9220
  646.9 43.8 %copy-start.58 = (f32[1,768]{1,0:T(1,128)S(1)}, f32[1,768]{1,0:T(1,128)}, u32[]{:S(2)}) copy-start(f32[1,768]{1,0:T(1,128)} %reshape.654) | copy-start | bytes 9220
  646.9 43.8 %copy-start.59 = (f32[1,768]{1,0:T(1,128)S(1)}, f32[1,768]{1,0:T(1,128)}, u32[]{:S(2)}) copy-start(f32[1,768]{1,0:T(1,128)} %reshape.651) | copy-start | bytes 9220
  646.9 43.8 %copy-start.60 = (f32[1,768]{1,0:T(1,128)S(1)}, f32[1,768]{1,0:T(1,128)}, u32[]{:S(2)}) copy-start(f32[1,768]{1,0:T(1,128)} %reshape.652) | copy-start | bytes 9220
  647.0 44.4 %copy-start.38 = (f32[1920]{0:T(1024)S(1)}, f32[1920]{0:T(1024)}, u32[]{:S(2)}) copy-start(f32[1920]{0:T(1024)} %copy-done.37) | copy-start | bytes 23044
  647.0 44.4 %copy-start.41 = (f32[768]{0:T(1024)S(1)}, f32[768]{0:T(1024)}, u32[]{:S(2)}) copy-start(f32[768]{0:T(1024)} %copy-done.40) | copy-start | bytes 9220
  697.6 60.9 %copy-start.49 = (f32[768]{0:T(1024)S(1)}, f32[768]{0:T(1024)}, u32[]{:S(2)}) copy-start(f32[768]{0:T(1024)} %copy-done.48) | copy-start | bytes 9220
  697.6 60.9 %copy-start.47 = (f32[768]{0:T(1024)S(1)}, f32[768]{0:T(1024)}, u32[]{:S(2)}) copy-start(f32[768]{0:T(1024)} %copy-done.46) | copy-start | bytes 9220
  697.6 61.0 %copy-start.45 = (f32[768]{0:T(1024)S(1)}, f32[768]{0:T(1024)}, u32[]{:S(2)}) copy-start(f32[768]{0:T(1024)} %get-tuple-element.23) | copy-start | bytes 9220
  697.6 61.0 %copy-start.43 = (f32[768]{0:T(1024)S(1)}, f32[768]{0:T(1024)}, u32[]{:S(2)}) copy-start(f32[768]{0:T(1024)} %get-tuple-element.27) | copy-start | bytes 9220
  759.2 16.1 %copy-start.13 = (f32[1,192,192]{2,1,0:T(8,128)S(1)}, f32[1,192,192]{2,1,0:T(8,128)}, u32[]{:S(2)}) copy-start(f32[1,192,192]{2,1,0:T(8,128)} %param.32) | copy-start | bytes 442372
  759.2 16.1 %copy-start.32 = (f32[1,192,192]{2,1,0:T(8,128)S(1)}, f32[1,192,192]{2,1,0:T(8,128)}, u32[]{:S(2)}) copy-start(f32[1,192,192]{2,1,0:T(8,128)} %param.41) | copy-start | bytes 442372
  759.2 16.0 %copy-start.33 = (f32[1,192,192]{2,1,0:T(8,128)S(1)}, f32[1,192,192]{2,1,0:T(8,128)}, u32[]{:S(2)}) copy-start(f32[1,192,192]{2,1,0:T(8,128)} %param.40) | copy-start | bytes 442372
  759.2 16.9 %copy-start.16 = (f32[1,192,768]{2,1,0:T(8,128)S(1)}, f32[1,192,768]{2,1,0:T(8,128)}, u32[]{:S(2)}) copy-start(f32[1,192,768]{2,1,0:T(8,128)} %param.43) | copy-start | bytes 1769476
  759.3 16.9 %copy-start.17 = (f32[1,192,768]{2,1,0:T(8,128)S(1)}, f32[1,192,768]{2,1,0:T(8,128)}, u32[]{:S(2)}) copy-start(f32[1,192,768]{2,1,0:T(8,128)} %param.42) | copy-start | bytes 1769476
  (27 other events, 96.7 us)
Sparse Core Ops, SparseCore 0:
  33.9 42.6 all-reduce.8
  79.0 34.2 all-reduce.10
  243.3 35.7 reduce-scatter.16
  282.1 17.5 reduce-scatter.12
  351.3 34.1 all-reduce.12
  423.4 34.1 all-reduce.14
  546.0 30.0 reduce-scatter.18
  579.1 17.6 reduce-scatter.14
